TPU v7x, 32 devices: a whole 2x2x4 slice. The times are simulated.
32 devices in a mesh: groups: 2 (over y), wide: 4 (over z), expert: 2 (over x), inner: 2 (over core).
Axes of the slice: x: 2, y: 2, z: 4, core: 2. Of those that a mesh axis runs over, the one named last changes fastest.
Arguments:
- candidates: bfloat16 [4096, 1024], P(('groups', 'wide')), parts along dimension 0, may hold values from -6 to 6
- gate_weight: bfloat16 [1024, 128], replicated
- expert_in: bfloat16 [32, 1024, 2048], P('expert', None, ('wide', 'inner')), may hold values from -0.1875 to 0.1875
- expert_out: bfloat16 [32, 256, 2048], P('expert', None, ('wide', 'inner')), may hold values from -0.125 to 0.125
- norm_gain: bfloat16 [1024], replicated, may hold values from 0.099609375 to 1.8984375
- query_weight: bfloat16 [1024, 1024], P(None, ('expert', 'inner'))
- key_weight: bfloat16 [1024, 1024], P(None, ('expert', 'inner'))
- value_weight: bfloat16 [1024, 1024], P(None, ('expert', 'inner')), may hold values from -0.1875 to 0.1875
- task_weight: bfloat16 [1024, 4], replicated, may hold values from -0.1875 to 0.1875
- attn_weight: bfloat16 [1024, 4], P(('expert', 'inner')), may hold values from -0.75 to 0.75
- request_of: int32 [4096], P(('groups', 'wide')), parts along dimension 0, may hold values from 0 to 7, as said below
Outputs:
- scores: float32 [4096, 4], P(('groups', 'wide')), parts along dimension 0
There are 2 independent parts, one for each index of `groups`. A program takes and returns all parts, laid end to end along the dimension named above; an argument that names none is the same for every part. Nothing has to cross between parts.
Inputs may be any that keep to these rules, and one draw needn't show every extreme that they name: `request_of`: candidates of a request arrive in any order over the shards. Among the 512 candidates of one shard of wide, no request has more than 128; one request has exactly 128 in every shard.
All inputs are finite; a program needn't handle non-finite values.
Results may differ from a plain program's by a relative error of at most 0.0051.
Values may be sent and summed in bfloat16 or wider, within the bound.
A program may use at most 128 MiB of HBM per device.

v0:
```python
import math

import jax
import jax.numpy as jnp
from jax import lax
from jax.sharding import PartitionSpec as P

HD = 64
REQ_DEV = 2


def local(
    candidates,
    gate_weight,
    expert_in,
    expert_out,
    norm_gain,
    query_weight,
    key_weight,
    value_weight,
    task_weight,
    attn_weight,
    request_of,
):
    count_rows = candidates.shape[0]
    n_wide = lax.axis_size("wide")
    tasks = task_weight.shape[1]
    experts_all = gate_weight.shape[1] // tasks
    local_experts = expert_in.shape[0]
    out_width = expert_out.shape[1]
    logits = jnp.dot(candidates, gate_weight, preferred_element_type=jnp.float32).reshape(
        count_rows, tasks, experts_all
    )
    gates = jax.nn.softmax(logits, axis=-1)
    own_gates = lax.dynamic_slice_in_dim(
        gates, lax.axis_index("expert") * local_experts, local_experts, 2
    )
    hidden_all = jax.nn.relu(
        jnp.einsum(
            "rd,edf->ref",
            candidates,
            lax.all_gather(expert_in, "wide", axis=2, tiled=True),
            preferred_element_type=jnp.float32,
        )
    ).astype(jnp.bfloat16)
    outputs = jnp.einsum(
        "ref,ejf->rej",
        hidden_all,
        lax.all_gather(expert_out, "wide", axis=2, tiled=True),
        preferred_element_type=jnp.float32,
    )
    partial_mix = jnp.einsum(
        "rte,rej->rtj", own_gates, outputs, precision=lax.Precision.HIGHEST
    ).reshape(count_rows, tasks * out_width)
    gain = norm_gain.astype(jnp.float32)
    mixed = lax.psum(partial_mix, ("expert", "inner"))
    center = jnp.mean(mixed, axis=1, keepdims=True)
    spread = jnp.mean(jnp.square(mixed - center), axis=1, keepdims=True)
    normed = ((mixed - center) * lax.rsqrt(spread + 1e-05) * gain).astype(jnp.bfloat16)
    queries = jnp.dot(normed, query_weight, preferred_element_type=jnp.float32).astype(jnp.bfloat16)
    keys = jnp.dot(normed, key_weight, preferred_element_type=jnp.float32).astype(jnp.bfloat16)
    values = jnp.dot(normed, value_weight, preferred_element_type=jnp.float32).astype(jnp.bfloat16)
    packed = jnp.concatenate([queries, keys, values], axis=1)
    head_width = query_weight.shape[1]
    heads_here = head_width // HD
    requests_all = REQ_DEV * n_wide
    capacity = 2 * count_rows // requests_all
    slots_all = requests_all * capacity
    member = request_of[:, None] == jnp.arange(requests_all, dtype=jnp.int32)[None, :]
    running = jnp.cumsum(member.astype(jnp.int32), axis=0)
    rank = jnp.sum(jnp.where(member, running, 0), axis=1) - 1
    slot = request_of * capacity + rank
    placing = (slot[None, :] == jnp.arange(slots_all, dtype=jnp.int32)[:, None]).astype(
        jnp.bfloat16
    )
    outgoing = jnp.dot(placing, packed, preferred_element_type=jnp.float32).astype(jnp.bfloat16)
    outgoing = outgoing.reshape(n_wide, REQ_DEV, capacity, 3 * head_width)
    present = jnp.max(placing, axis=1).reshape(n_wide, REQ_DEV, capacity)
    factor = 1.0 / math.sqrt(HD)
    span = n_wide * capacity
    block = lax.all_to_all(outgoing, "wide", split_axis=0, concat_axis=0, tiled=True)
    flags = lax.all_to_all(present, "wide", split_axis=0, concat_axis=0, tiled=True)
    items = block.shape[1]
    arranged = jnp.transpose(block, (1, 0, 2, 3)).reshape(items, span, 3, heads_here, HD)
    live = jnp.transpose(flags, (1, 0, 2)).reshape(items, span) > 0
    affinity = (
        jnp.einsum(
            "iqhd,ikhd->ihqk",
            arranged[:, :, 0],
            arranged[:, :, 1],
            preferred_element_type=jnp.float32,
        )
        * factor
    )
    affinity = jnp.where(live[:, None, None, :], affinity, -1e30)
    highest = jnp.max(affinity, axis=-1, keepdims=True)
    powers = jnp.exp(affinity - highest)
    probs = (powers / jnp.sum(powers, axis=-1, keepdims=True)).astype(jnp.bfloat16)
    context = jnp.einsum(
        "ihqk,ikhd->iqhd", probs, arranged[:, :, 2], preferred_element_type=jnp.float32
    )
    context = context.astype(jnp.bfloat16).reshape(items, span, head_width)
    term = jnp.einsum("iqc,ct->iqt", context, attn_weight, preferred_element_type=jnp.float32)
    arrived = jnp.transpose(term.reshape(items, n_wide, capacity, tasks), (1, 0, 2, 3))
    returned = lax.all_to_all(arrived, "wide", split_axis=0, concat_axis=0, tiled=True)
    per_row = jnp.take(returned.reshape(slots_all, tasks), slot, axis=0)
    attention = lax.psum(per_row, ("expert", "inner"))
    return jnp.dot(normed, task_weight, preferred_element_type=jnp.float32) + attention


def solution(mesh):
    return jax.shard_map(
        local,
        mesh=mesh,
        in_specs=(
            P(("groups", "wide"), None),
            P(),
            P("expert", None, ("wide", "inner")),
            P("expert", None, ("wide", "inner")),
            P(),
            P(None, ("expert", "inner")),
            P(None, ("expert", "inner")),
            P(None, ("expert", "inner")),
            P(),
            P(("expert", "inner"), None),
            P(("groups", "wide")),
        ),
        out_specs=P(("groups", "wide"), None),
        check_vma=False,
    )
```

profile of v0, /device:TPU:9, one launch (start us, length us, event | category | flops | bytes accessed | tf_op | source)
XLA Modules:
  0.0 906.5 jit_solution(17711067642507584241)
XLA Ops:
  6.5 0.7 all-gather.5.cloned.1.call-update
  7.3 0.7 all-gather.3.cloned.1.call-update
  8.3 0.5 bitcast_reduce_fusion
  8.8 0.9 copy.39
  10.0 2.5 fusion.42
  12.5 143.7 %all-gather.5.cloned.1.call-done = bf16[16,256,1024]{2,1,0:T(8,128)(2,1)} async-done(((bf16[16,256,256]{2,1,0:T(8,128)(2,1)}), bf16[16,256,1024]{2,1,0:T(8,128)(2,1)}) %all-gather.5.cloned.1.call-update) | async-done | bytes 8388624 | tf_op jit(solution)/shard_map/all_gather | solution.py:49
  156.3 560.7 %all-gather.3.cloned.1.call-done = bf16[16,1024,1024]{2,1,0:T(8,128)(2,1)} async-done(((bf16[16,1024,256]{2,1,0:T(8,128)(2,1)}), bf16[16,1024,1024]{2,1,0:T(8,128)(2,1)}) %all-gather.3.cloned.1.call-update) | async-done | bytes 33554448 | tf_op jit(solution)/shard_map/all_gather | solution.py:42
  716.9 27.7 %fusion.12 = f32[512,16,256]{2,0,1:T(8,128)} fusion(bf16[16,256,1024]{2,1,0:T(8,128)(2,1)} %all-gather.5.cloned.1.call-done, bf16[16,1024,1024]{2,1,0:T(8,128)(2,1)} %all-gather.3.cloned.1.call-done, bf16[512,1024]{1,0:T(8,128)(2,1)S(1)} %copy-done), kind=kOutput, calls=%fused_computation.16 | convolution fusion | flops 21491613696 | bytes 51380224 | tf_op jit(solution)/shard_map/ref,ejf->rej/dot_general | solution.py:46
  744.6 12.7 %fusion.5 = f32[512,4,256]{2,1,0:T(4,128)S(1)} fusion(f32[512,16,256]{2,0,1:T(8,128)} %fusion.12, f32[512,4,32]{2,1,0:T(4,128)S(1)} %get-tuple-element.8, s32[]{:T(128)S(6)} %select_n.20, f32[512,4]{1,0:T(8,128)S(1)} %get-tuple-element.7), kind=kOutput, calls=%fused_computation.6 | convolution fusion | flops 100696064 | bytes 10756100 | tf_op jit(solution)/shard_map/rte,rej->rtj/dot_general | solution.py:52
  757.3 1.8 copy.57
  759.1 1.1 reduce-window.6
  760.6 0.9 fusion.19
  761.5 5.7 all-to-all-start.1
  767.2 44.3 %all-reduce.2.cloned.1.call-done = f32[512,1024]{1,0:T(8,128)} async-done(((f32[512,1024]{1,0:T(8,128)}), f32[512,1024]{1,0:T(8,128)}) %all-reduce.2.cloned.1.call-update) | async-done | bytes 2097168 | tf_op jit(solution)/shard_map/psum | solution.py:56
  811.5 1.9 reduce_sum.46
  814.1 1.0 copy-done.3
  815.4 0.5 convolution_convert_fusion
  815.9 0.5 convolution_convert_fusion.1
  816.9 2.2 fusion.15
  819.1 2.6 copy.42
  821.7 4.6 all-to-all-start
  826.3 32.9 %all-to-all-done = bf16[4,2,128,768]{2,3,1,0:T(8,128)(2,1)} async-done(((bf16[4,2,128,768]{2,3,1,0:T(8,128)(2,1)}), bf16[4,2,128,768]{2,3,1,0:T(8,128)(2,1)}, u32[]{:S(2)}, u32[]{:S(2)}) %all-to-all-start) | async-done | bytes 1572896 | tf_op jit(solution)/shard_map/all_to_all | solution.py:81
  859.2 3.8 copy.43
  863.0 3.6 reshape.73
  866.6 7.6 fusion.43
  874.2 4.5 fusion.17
  879.0 0.6 copy.49
  879.7 7.0 all-to-all-start.2
  886.6 3.4 all-to-all-done.2
  890.2 1.0 gather_fusion
  891.4 7.6 psum.15
  899.0 1.0 convolution_add_fusion
  (49 shorter events, 3.2 us)
Async XLA Ops:
  6.5 1.5 copy-start
  6.5 149.7 %all-gather.5.cloned.1.call-start = ((), (), s32[]{:S(2)}) async-start(), calls=%async_computation.4 | async-start | bytes 10485760 | tf_op jit(solution)/shard_map/all_gather | solution.py:49
  7.3 1.0 copy-start.7
  7.3 709.7 %all-gather.3.cloned.1.call-start = ((), (), s32[]{:S(2)}) async-start(), calls=%async_computation.3 | async-start | bytes 41943040 | tf_op jit(solution)/shard_map/all_gather | solution.py:42
  8.0 803.5 %all-reduce.2.cloned.1.call-start = ((), (), s32[]{:S(2)}) async-start(), calls=%async_computation.5 | async-start | bytes 4194304 | tf_op jit(solution)/shard_map/psum | solution.py:56
  757.3 1.8 copy-start.8
  757.3 9.9 %copy-start.10 = (bf16[1024]{0:T(1024)(128)(2,1)S(1)}, bf16[1024]{0:T(1024)(128)(2,1)}, u32[]{:S(2)}) copy-start(bf16[1024]{0:T(1024)(128)(2,1)} %param.15) | copy-start | bytes 6148
  761.5 60.2 %all-to-all-start.1 = ((bf16[4,2,128]{2,1,0:T(2,128)(2,1)}), bf16[4,2,128]{2,1,0:T(2,128)(2,1)S(1)}, u32[]{:S(2)}, u32[]{:S(2)}) async-start(bf16[4,2,128]{2,1,0:T(2,128)(2,1)} %bitcast.9), calls=%async_computation.1 | async-start | bytes 4096 | tf_op jit(solution)/shard_map/all_to_all | solution.py:82
  811.5 2.2 copy-start.2
  813.4 1.7 copy-start.3
  813.4 2.0 copy-start.4
  813.7 2.2 copy-start.5
  815.1 1.3 copy-start.6
  821.7 37.4 %all-to-all-start = ((bf16[4,2,128,768]{2,3,1,0:T(8,128)(2,1)}), bf16[4,2,128,768]{2,3,1,0:T(8,128)(2,1)}, u32[]{:S(2)}, u32[]{:S(2)}) async-start(bf16[4,2,128,768]{2,3,1,0:T(8,128)(2,1)} %copy.42), calls=%async_computation | async-start | bytes 3145728 | tf_op jit(solution)/shard_map/all_to_all | solution.py:81
  874.2 4.6 copy-start.11
  874.2 25.8 %copy-start.1 = (bf16[512,1024]{1,0:T(8,128)(2,1)S(1)}, bf16[512,1024]{1,0:T(8,128)(2,1)}, u32[]{:S(2)}) copy-start(bf16[512,1024]{1,0:T(8,128)(2,1)} %param.11) | copy-start | bytes 3145732
  878.7 20.3 %copy-start.9 = (bf16[1024,4]{0,1:T(4,128)(2,1)S(1)}, bf16[1024,4]{0,1:T(4,128)(2,1)}, u32[]{:S(2)}) copy-start(bf16[1024,4]{0,1:T(4,128)(2,1)} %param.19) | copy-start | bytes 24580
  879.7 10.3 %all-to-all-start.2 = ((f32[4,2,128,4]{2,3,1,0:T(4,128)}), f32[4,2,128,4]{2,3,1,0:T(4,128)S(1)}, u32[]{:S(2)}, u32[]{:S(2)}) async-start(f32[4,2,128,4]{2,3,1,0:T(4,128)} %copy.49), calls=%async_computation.2 | async-start | bytes 32768 | tf_op jit(solution)/shard_map/all_to_all | solution.py:105
Sparse Core Ops, SparseCore 0:
  8.9 147.3 all-gather.4
  157.8 559.0 all-gather.2
  759.2 52.2 all-reduce.1
where the time goes:
time: 909 us; the launch traced here: 907 us
  waiting for transfers between devices  786 us (86%)
  matrix products  57.8 us (6%)
  starting transfers between devices  17.3 us (2%)
  local copies, waits for them, and re-layouts  16.8 us (2%)
  between operations  13.3 us (1%)
    all_gather x1, waiting for transfers between devices, local(): lax.all_gather(expert_in, 'wide', axis=2, tiled=True)  561 us
    all_gather x1, waiting for transfers between devices, local(): lax.all_gather(expert_out, 'wide', axis=2, tiled=True)  144 us
    psum x1, waiting for transfers between devices, local(): mixed = lax.psum(partial_mix, ('expert', 'inner'))  44.3 us
    all_to_all x1, waiting for transfers between devices, local(): lax.all_to_all(outgoing, 'wide', split_axis=0, concat_axis=0, tiled=True)  32.9 us
    dot_general x1, matrix products, local(): jnp.einsum('ref,ejf->rej', hidden_all, lax.all_gather(expert_out, 'wide',...  27.7 us
  transfers between devices with their start and end apart: 6, of which 5 were waited for; matrix products, arithmetic and copies ran while one was open for 2% of the time, Pallas kernels for 0%

commit v1 on v0

v1 whole, which is shorter than its diff:
```python
import functools
import math

import jax
import jax.numpy as jnp
from jax import lax
from jax.experimental import pallas as pl
from jax.experimental.pallas import tpu as pltpu
from jax.sharding import PartitionSpec as P

HD = 64
ALL = ("wide", "expert", "inner")
VMEM_LIMIT = 60 * 1024 * 1024


def expert_kernel(tasks, x_ref, gate_ref, win_ref, wout_ref, out_ref, acc_ref):
    rows = x_ref.shape[0]
    columns = gate_ref.shape[1]
    experts_all = columns // tasks
    held, _, _ = win_ref.shape
    width = wout_ref.shape[1]
    x = x_ref[...]
    logits = jnp.dot(x, gate_ref[...], preferred_element_type=jnp.float32)
    task = lax.broadcasted_iota(jnp.int32, (rows, columns), 1) // experts_all
    top = jnp.zeros_like(logits)
    for t in range(tasks):
        high = jnp.max(jnp.where(task == t, logits, -jnp.inf), axis=1, keepdims=True)
        top = jnp.where(task == t, high, top)
    powers = jnp.exp(logits - top)
    total = jnp.ones_like(logits)
    for t in range(tasks):
        part = jnp.sum(jnp.where(task == t, powers, 0.0), axis=1, keepdims=True)
        total = jnp.where(task == t, part, total)
    gates = powers / total
    shift = lax.rem(columns - lax.axis_index("expert") * held, columns)
    gates = pltpu.roll(gates, shift, 1)
    together = min(4, held)
    for first in range(0, held, together):
        made = []
        for e in range(first, first + together):
            hidden = jnp.maximum(
                jnp.dot(x, win_ref[e], preferred_element_type=jnp.float32), 0.0
            ).astype(jnp.bfloat16)
            made.append(
                lax.dot_general(
                    hidden,
                    wout_ref[e],
                    (((1,), (1,)), ((), ())),
                    preferred_element_type=jnp.float32,
                )
            )
        for t in range(tasks):
            piece = None
            for j, output in enumerate(made):
                lane = t * experts_all + first + j
                term = gates[:, lane : lane + 1] * output
                piece = term if piece is None else piece + term
            span = slice(t * width, (t + 1) * width)
            if first > 0:
                piece = piece + acc_ref[:, span]
            if first + together < held:
                acc_ref[:, span] = piece
            else:
                out_ref[:, span] = piece.astype(out_ref.dtype)


def run_experts(x, gate_weight, expert_in, expert_out, tasks):
    rows, depth = x.shape
    held, _, units = expert_in.shape
    width = expert_out.shape[1]
    block = min(256, rows)
    return pl.pallas_call(
        functools.partial(expert_kernel, tasks),
        grid=(rows // block,),
        in_specs=[
            pl.BlockSpec((block, depth), lambda i: (i, 0)),
            pl.BlockSpec(gate_weight.shape, lambda i: (0, 0)),
            pl.BlockSpec(expert_in.shape, lambda i: (0, 0, 0), pipeline_mode=pl.Buffered(1)),
            pl.BlockSpec(expert_out.shape, lambda i: (0, 0, 0), pipeline_mode=pl.Buffered(1)),
        ],
        out_specs=pl.BlockSpec((block, tasks * width), lambda i: (i, 0)),
        out_shape=jax.ShapeDtypeStruct((rows, tasks * width), jnp.float32),
        scratch_shapes=[pltpu.VMEM((block, tasks * width), jnp.float32)],
        compiler_params=pltpu.CompilerParams(vmem_limit_bytes=VMEM_LIMIT),
    )(x, gate_weight, expert_in, expert_out)


def attention_kernel(q_ref, k_ref, v_ref, own_ref, all_ref, weight_ref, out_ref):
    same = own_ref[...] == all_ref[...]
    factor = 1.0 / math.sqrt(HD)
    result = None
    for first in range(0, q_ref.shape[1], HD):
        span = slice(first, first + HD)
        affinity = (
            lax.dot_general(
                q_ref[:, span],
                k_ref[:, span],
                (((1,), (1,)), ((), ())),
                preferred_element_type=jnp.float32,
            )
            * factor
        )
        affinity = jnp.where(same, affinity, -1e30)
        highest = jnp.max(affinity, axis=1, keepdims=True)
        powers = jnp.exp(affinity - highest)
        total = jnp.sum(powers, axis=1, keepdims=True)
        context = jnp.dot(
            powers.astype(jnp.bfloat16), v_ref[:, span], preferred_element_type=jnp.float32
        )
        context = (context / total).astype(jnp.bfloat16)
        term = jnp.dot(context, weight_ref[span, :], preferred_element_type=jnp.float32)
        result = term if result is None else result + term
    out_ref[...] = result


def run_attention(q, k, v, own, every, weight):
    rows, width = q.shape
    keys = k.shape[0]
    tasks = weight.shape[1]
    block = min(128, rows)
    return pl.pallas_call(
        attention_kernel,
        grid=(rows // block,),
        in_specs=[
            pl.BlockSpec((block, width), lambda i: (i, 0)),
            pl.BlockSpec((keys, width), lambda i: (0, 0)),
            pl.BlockSpec((keys, width), lambda i: (0, 0)),
            pl.BlockSpec((block, 1), lambda i: (i, 0)),
            pl.BlockSpec((1, keys), lambda i: (0, 0)),
            pl.BlockSpec((width, tasks), lambda i: (0, 0)),
        ],
        out_specs=pl.BlockSpec((block, tasks), lambda i: (i, 0)),
        out_shape=jax.ShapeDtypeStruct((rows, tasks), jnp.float32),
        compiler_params=pltpu.CompilerParams(vmem_limit_bytes=VMEM_LIMIT),
    )(q, k, v, own, every, weight)


def local(
    candidates,
    gate_weight,
    expert_in,
    expert_out,
    norm_gain,
    query_weight,
    key_weight,
    value_weight,
    task_weight,
    attn_weight,
    request_of,
):
    rows = candidates.shape[0]
    tasks = task_weight.shape[1]
    share = rows // (lax.axis_size("expert") * lax.axis_size("inner"))
    spot = lax.axis_index("expert") * lax.axis_size("inner") + lax.axis_index("inner")
    wide = lax.axis_index("wide")
    requests = lax.all_gather(request_of, "wide", axis=0, tiled=True)
    quarter = lax.dynamic_slice_in_dim(candidates, spot * share, share, 0)
    everyone = lax.all_gather(quarter, ALL, axis=0, tiled=True)
    partial_mix = run_experts(everyone, gate_weight, expert_in, expert_out, tasks)
    mixed = lax.psum_scatter(partial_mix, ALL, scatter_dimension=0, tiled=True)
    center = jnp.mean(mixed, axis=1, keepdims=True)
    spread = jnp.mean(jnp.square(mixed - center), axis=1, keepdims=True)
    gain = norm_gain.astype(jnp.float32)
    normed = ((mixed - center) * lax.rsqrt(spread + 1e-05) * gain).astype(jnp.bfloat16)
    normed_all = lax.all_gather(normed, ALL, axis=0, tiled=True)
    own = lax.dynamic_slice_in_dim(normed_all, wide * rows, rows, 0)
    queries = jnp.dot(own, query_weight, preferred_element_type=jnp.float32).astype(jnp.bfloat16)
    keys = jnp.dot(normed_all, key_weight, preferred_element_type=jnp.float32).astype(jnp.bfloat16)
    values = jnp.dot(normed_all, value_weight, preferred_element_type=jnp.float32).astype(
        jnp.bfloat16
    )
    term = run_attention(
        queries, keys, values, request_of[:, None], requests[None, :], attn_weight
    )
    attention = lax.psum(term, ("expert", "inner"))
    return jnp.dot(own, task_weight, preferred_element_type=jnp.float32) + attention


def solution(mesh):
    return jax.shard_map(
        local,
        mesh=mesh,
        in_specs=(
            P(("groups", "wide"), None),
            P(),
            P("expert", None, ("wide", "inner")),
            P("expert", None, ("wide", "inner")),
            P(),
            P(None, ("expert", "inner")),
            P(None, ("expert", "inner")),
            P(None, ("expert", "inner")),
            P(),
            P(("expert", "inner"), None),
            P(("groups", "wide")),
        ),
        out_specs=P(("groups", "wide"), None),
        check_vma=False,
    )
```

time: 909 us -> 328 us (0.36)
  waiting for transfers between devices: 786 us -> 194 us
  Pallas kernels: 0 us -> 76.4 us
  matrix products: 57.8 us -> 9.67 us
  starting transfers between devices: 17.3 us -> 0.09 us
  blocking collectives: 7.62 us -> 23.5 us
  local copies, waits for them, and re-layouts: 16.8 us -> 4.87 us
    all_gather x2, waiting for transfers between devices: 704 us -> 92.9 us  [the longest x1 53 us: local(): everyone = lax.all_gather(quarter, ALL, axis=0, tiled=True)]
    reduce_scatter x0 -> x1, waiting for transfers between devices: none -> 101 us  [local(): mixed = lax.psum_scatter(partial_mix, ALL, scatter_dimension=0, tiled=True)]
    pallas_call x0 -> x2, Pallas kernels: none -> 76.4 us  [the longest x1 62.8 us: run_experts(): pl.pallas_call(functools.partial(expert_kernel, tasks), grid=(rows // blo...]
    psum x1 -> x0, waiting for transfers between devices: 44.3 us -> none  [local(): mixed = lax.psum(partial_mix, ('expert', 'inner'))]
    dot_general x10 -> x4, matrix products: 50.2 us -> 9.67 us  [the longest x1 4.6 us: local(): jnp.dot(normed_all, value_weight, preferred_element_type=jnp.float32)]
    all_to_all x3 -> x0, waiting for transfers between devices: 36.2 us -> none  [the longest x1 32.9 us: local(): lax.all_to_all(outgoing, 'wide', split_axis=0, concat_axis=0, tiled=True)]
    all_to_all x3 -> x0, starting transfers between devices: 17.2 us -> none  [the longest x1 6.97 us: local(): lax.all_to_all(arrived, 'wide', split_axis=0, concat_axis=0, tiled=True)]
    all_gather x0 -> x1, blocking collectives: none -> 9.32 us  [local(): requests = lax.all_gather(request_of, 'wide', axis=0, tiled=True)]
  transfers between devices with their start and end apart: 6 -> 3, of which waited for: 5 -> 3; matrix products, arithmetic and copies ran while one was open for 2% -> 0% of each run, Pallas kernels for 0% -> 0%
where the time goes in v1:
time: 328 us; the launch traced here: 326 us
  waiting for transfers between devices  194 us (59%)
  Pallas kernels  76.4 us (23%)
  blocking collectives  23.5 us (7%)
  between operations  13.2 us (4%)
  matrix products  9.67 us (3%)
  local copies, waits for them, and re-layouts  4.87 us (1%)
  other arithmetic  4.32 us (1%)
    reduce_scatter x1, waiting for transfers between devices, local(): mixed = lax.psum_scatter(partial_mix, ALL, scatter_dimension=0, tiled=True)  101 us
    pallas_call x1, Pallas kernels, run_experts(): pl.pallas_call(functools.partial(expert_kernel, tasks), grid=(rows // blo...  62.8 us
    all_gather x1, waiting for transfers between devices, local(): everyone = lax.all_gather(quarter, ALL, axis=0, tiled=True)  53 us
    all_gather x1, waiting for transfers between devices, local(): normed_all = lax.all_gather(normed, ALL, axis=0, tiled=True)  39.9 us
    psum x1, blocking collectives, local(): attention = lax.psum(term, ('expert', 'inner'))  14.2 us
    pallas_call x1, Pallas kernels, run_attention(): pl.pallas_call(attention_kernel, grid=(rows // block,), in_specs=[pl.Bloc...  13.6 us
    all_gather x1, blocking collectives, local(): requests = lax.all_gather(request_of, 'wide', axis=0, tiled=True)  9.32 us
  transfers between devices with their start and end apart: 3, of which 3 were waited for; matrix products, arithmetic and copies ran while one was open for 0% of the time, Pallas kernels for 0%

profile of v1, /device:TPU:9, one launch (start us, length us, event | category | flops | bytes accessed | tf_op | source)
XLA Modules:
  0.0 325.8 jit_solution(12341996595835988965)
XLA Ops:
  6.5 0.0 copy-start
  6.5 0.0 all-gather.4.cloned.1.call-start
  6.5 1.2 copy-done
  7.8 0.7 constant_dynamic-slice_fusion
  8.5 0.0 all-gather.4.cloned.1.call-update
  8.5 0.0 reduce-scatter.2.cloned.1.call-start
  8.6 53.0 %all-gather.4.cloned.1.call-done.x_ref = bf16[2048,1024]{1,0:T(8,128)(2,1)} async-done(((bf16[128,1024]{1,0:T(8,128)(2,1)}), bf16[2048,1024]{1,0:T(8,128)(2,1)}) %all-gather.4.cloned.1.call-update) | async-done | bytes 4194320 | tf_op jit(solution)/shard_map/all_gather | solution.py:158
  61.5 62.8 %shard_map.109 = f32[2048,1024]{1,0:T(8,128)} custom-call(bf16[2048,1024]{1,0:T(8,128)(2,1)} %all-gather.4.cloned.1.call-done.x_ref, bf16[1024,128]{1,0:T(8,128)(2,1)} %gate_ref.1, bf16[16,1024,256]{2,1,0:T(8,128)(2,1)} %win_ref.1, bf16[16,256,256]{2,1,0:T(8,128)(2,1)} %wout_ref.1), custom_call_target="tpu_custom_call" | custom-call | tf_op jit(solution)/shard_map/pallas_call | solution.py:72
  124.3 0.0 copy-start.6
  124.3 0.0 reduce-scatter.2.cloned.1.call-update
  124.3 0.0 all-gather.6.cloned.1.call-start
  124.4 0.6 copy-done.4
  125.0 100.9 %reduce-scatter.2.cloned.1.call-done = f32[128,1024]{1,0:T(8,128)} async-done(((f32[2048,1024]{1,0:T(8,128)}), f32[128,1024]{1,0:T(8,128)}) %reduce-scatter.2.cloned.1.call-update) | async-done | bytes 524304 | tf_op jit(solution)/shard_map/reduce_scatter | solution.py:160
  225.8 1.2 reduce_sum.18
  227.0 1.2 multiply_reduce_fusion
  228.3 1.9 multiply_convert_fusion
  230.2 0.0 all-gather.6.cloned.1.call-update
  230.2 0.0 copy-done.3
  230.2 0.8 copy.23.own_ref
  231.1 0.0 copy-done.5
  231.1 0.7 copy.24.weight_ref
  231.8 9.3 %all-gather = s32[4,1,512]{2,1,0:T(1,128)} all-gather(s32[1,1,512]{2,1,0:T(1,128)S(1)} %bitcast.11), channel_id=1, replica_groups=mesh['groups'=2,'wide'=4,'expert'=2,'inner'=2] {'wide'}, dimensions={0}, use_global_device_ids=true | all-gather | bytes 10240 | tf_op jit(solution)/shard_map/all_gather | solution.py:156
  241.1 39.9 %all-gather.6.cloned.1.call-done = bf16[2048,1024]{1,0:T(8,128)(2,1)} async-done(((bf16[128,1024]{1,0:T(8,128)(2,1)}), bf16[2048,1024]{1,0:T(8,128)(2,1)}) %all-gather.6.cloned.1.call-update) | async-done | bytes 4194320 | tf_op jit(solution)/shard_map/all_gather | solution.py:165
  281.1 0.0 copy-done.6
  281.1 4.6 %convolution_convert_fusion.v_ref = bf16[2048,256]{1,0:T(8,128)(2,1)} fusion(bf16[2048,1024]{1,0:T(8,128)(2,1)} %all-gather.6.cloned.1.call-done, bf16[1024,256]{1,0:T(8,128)(2,1)S(1)} %copy-done.6), kind=kOutput, calls=%fused_computation | convolution fusion | flops 1074266112 | bytes 5767168 | tf_op jit(solution)/shard_map/dot_general | solution.py:169
  285.7 2.3 convolution_convert_fusion.1.k_ref
  287.9 1.2 convolution_convert_fusion.2.q_ref
  289.1 13.6 %shard_map.110 = f32[512,4]{1,0:T(8,128)} custom-call(bf16[512,256]{1,0:T(8,128)(2,1)} %convolution_convert_fusion.2.q_ref, bf16[2048,256]{1,0:T(8,128)(2,1)} %convolution_convert_fusion.1.k_ref, bf16[2048,256]{1,0:T(8,128)(2,1)} %convolution_convert_fusion.v_ref, s32[512,1]{1,0:T(8,128)} %copy.23.own_ref, s32[1,2048]{1,0:T(1,128)} %bitcast.9, ...), custom_call_target="tpu_custom_call" | custom-call | tf_op jit(solution)/shard_map/pallas_call | solution.py:121
  302.7 14.2 %psum.7 = f32[512,4]{1,0:T(8,128)S(1)} all-reduce(f32[512,4]{1,0:T(8,128)} %shard_map.110), channel_id=1, replica_groups=mesh['groups'=2,'wide'=4,'expert'=2,'inner'=2] {'expert','inner'}, use_global_device_ids=true, to_apply=%region_3.0 | all-reduce | flops 2048 | bytes 16384 | tf_op jit(solution)/shard_map/psum | solution.py:175
  316.9 0.0 copy-done.2
  316.9 1.6 convolution_add_fusion
  318.6 0.7 copy.26
  (13 shorter events, 0.0 us)
Async XLA Ops:
  6.5 1.2 copy-start
  6.5 55.0 %all-gather.4.cloned.1.call-start = ((), (), s32[]{:S(2)}) async-start(), calls=%async_computation.1 | async-start | bytes 4456448 | tf_op jit(solution)/shard_map/all_gather | solution.py:158
  8.5 217.3 %reduce-scatter.2.cloned.1.call-start = ((), (), s32[]{:S(2)}) async-start(), calls=%async_computation.2 | async-start | bytes 8912896 | tf_op jit(solution)/shard_map/reduce_scatter | solution.py:160
  124.3 0.7 copy-start.4
  124.3 105.9 %copy-start.3 = (s32[512]{0:T(512)S(1)}, s32[512]{0:T(512)}, u32[]{:S(2)}) copy-start(s32[512]{0:T(512)} %param.21) | copy-start | bytes 6148
  124.3 106.8 %copy-start.5 = (bf16[256,4]{0,1:T(4,128)(2,1)S(1)}, bf16[256,4]{0,1:T(4,128)(2,1)}, u32[]{:S(2)}) copy-start(bf16[256,4]{0,1:T(4,128)(2,1)} %param.20) | copy-start | bytes 6148
  124.3 156.8 %copy-start.6 = (bf16[1024,256]{1,0:T(8,128)(2,1)S(1)}, bf16[1024,256]{1,0:T(8,128)(2,1)}, u32[]{:S(2)}) copy-start(bf16[1024,256]{1,0:T(8,128)(2,1)} %param.18) | copy-start | bytes 1572868
  124.3 156.7 %all-gather.6.cloned.1.call-start = ((), (), s32[]{:S(2)}) async-start(), calls=%async_computation.3 | async-start | bytes 4456448 | tf_op jit(solution)/shard_map/all_gather | solution.py:165
  230.2 55.5 %copy-start.7 = (bf16[1024,256]{1,0:T(8,128)(2,1)S(1)}, bf16[1024,256]{1,0:T(8,128)(2,1)}, u32[]{:S(2)}) copy-start(bf16[1024,256]{1,0:T(8,128)(2,1)} %param.17) | copy-start | bytes 1572868
  281.1 4.6 %copy-start.1 = (bf16[2048,1024]{1,0:T(8,128)(2,1)S(1)}, bf16[2048,1024]{1,0:T(8,128)(2,1)}, u32[]{:S(2)}) copy-start(bf16[2048,1024]{1,0:T(8,128)(2,1)} %all-gather.6.cloned.1.call-done) | copy-start | bytes 12582916
  285.7 2.3 copy-start.8
  287.9 29.0 %copy-start.2 = (bf16[1024,4]{0,1:T(4,128)(2,1)S(1)}, bf16[1024,4]{0,1:T(4,128)(2,1)}, u32[]{:S(2)}) copy-start(bf16[1024,4]{0,1:T(4,128)(2,1)} %param.19) | copy-start | bytes 24580
Sparse Core Ops, SparseCore 0:
  9.5 51.9 all-gather.3
  124.5 101.3 reduce-scatter.1
  230.3 50.6 all-gather.5

commit v2 on v1

--- a/solution.py
+++ b/solution.py
@@ -11,6 +11,266 @@
 HD = 64
 ALL = ("wide", "expert", "inner")
 VMEM_LIMIT = 60 * 1024 * 1024
+
+
+MESH = pl.DeviceIdType.MESH
+
+
+def place():
+    return tuple(lax.axis_index(a) for a in ALL), tuple(lax.axis_size(a) for a in ALL)
+
+
+def turn(start, step, size):
+    return lax.rem(start + step, size)
+
+
+def greet():
+    mine, sizes = place()
+    barrier = pltpu.get_barrier_semaphore()
+    for axis, here, size in zip(ALL, mine, sizes):
+        for step in range(1, size):
+            pl.semaphore_signal(
+                barrier, inc=1, device_id={axis: turn(here, step, size)}, device_id_type=MESH
+            )
+    pl.semaphore_wait(barrier, sum(sizes) - len(sizes))
+
+
+def gather_kernel(with_ids, *refs):
+    if with_ids:
+        own_ref, id_ref, out_ref, ids_ref, recv, send_z, send_x, send_c, local_sem, id_r, id_s = refs
+    else:
+        own_ref, out_ref, recv, send_z, send_x, send_c, local_sem = refs
+    (z, x, c), (nz, nx, nc) = place()
+    greet()
+
+    def copy(src, zs, xs, cs, sem, axis, target):
+        return pltpu.make_async_remote_copy(
+            src_ref=src,
+            dst_ref=out_ref.at[zs, cs, xs],
+            send_sem=sem,
+            recv_sem=recv.at[zs, cs, xs],
+            device_id={axis: target},
+            device_id_type=MESH,
+        )
+
+    def arrived(zs, xs, cs):
+        copy(out_ref.at[zs, cs, xs], zs, xs, cs, send_z.at[0], "inner", turn(c, 1, nc)).wait_recv()
+
+    sent = []
+
+    def push(*what):
+        item = copy(*what)
+        item.start()
+        sent.append(item)
+
+    def spread_x(src, k, zs):
+        for step in range(1, nx):
+            push(src, zs, x, c, send_x.at[k, step - 1], "expert", turn(x, step, nx))
+
+    def spread_c(src, k, j, zs, xs):
+        for step in range(1, nc):
+            push(src, zs, xs, c, send_c.at[k, j, step - 1], "inner", turn(c, step, nc))
+
+    for step in range(1, nz):
+        push(own_ref, z, x, c, send_z.at[step - 1], "wide", turn(z, step, nz))
+    spread_x(own_ref, 0, z)
+    spread_c(own_ref, 0, 0, z, x)
+    keep = pltpu.make_async_copy(own_ref, out_ref.at[z, c, x], local_sem.at[0])
+    keep.start()
+    if with_ids:
+        id_copies = []
+        for step in range(1, nz):
+            item = pltpu.make_async_remote_copy(
+                src_ref=id_ref,
+                dst_ref=ids_ref.at[z],
+                send_sem=id_s.at[step - 1],
+                recv_sem=id_r.at[z],
+                device_id={"wide": turn(z, step, nz)},
+                device_id_type=MESH,
+            )
+            item.start()
+            id_copies.append(item)
+        ids_ref[z] = id_ref[...]
+
+    def pass_x(k):
+        zs = turn(z, k, nz)
+        for step in range(1, nx):
+            xs = turn(x, step, nx)
+            arrived(zs, xs, c)
+            spread_c(out_ref.at[zs, c, xs], k, step, zs, xs)
+
+    for k in range(1, nz):
+        zs = turn(z, k, nz)
+        arrived(zs, x, c)
+        spread_x(out_ref.at[zs, c, x], k, zs)
+        spread_c(out_ref.at[zs, c, x], k, 0, zs, x)
+        pass_x(k - 1)
+    pass_x(nz - 1)
+    for k in range(nz):
+        for j in range(nx):
+            for step in range(1, nc):
+                arrived(turn(z, k, nz), turn(x, j, nx), turn(c, step, nc))
+    for item in sent:
+        item.wait_send()
+    keep.wait()
+    if with_ids:
+        for step in range(1, nz):
+            zs = turn(z, step, nz)
+            pltpu.make_async_remote_copy(
+                src_ref=id_ref,
+                dst_ref=ids_ref.at[zs],
+                send_sem=id_s.at[step - 1],
+                recv_sem=id_r.at[zs],
+                device_id={"wide": zs},
+                device_id_type=MESH,
+            ).wait_recv()
+        for item in id_copies:
+            item.wait_send()
+
+
+def run_gather(own, ids, collective):
+    nz, nx, nc = (lax.axis_size(a) for a in ALL)
+    dma = pltpu.SemaphoreType.DMA
+    with_ids = ids is not None
+    shape = jax.ShapeDtypeStruct((nz, nc, nx) + own.shape, own.dtype)
+    vmem = pl.BlockSpec(memory_space=pltpu.VMEM)
+    anywhere = pl.BlockSpec(memory_space=pl.ANY)
+    scratch = [
+        dma((nz, nc, nx)),
+        dma((max(nz - 1, 1),)),
+        dma((nz, max(nx - 1, 1))),
+        dma((nz, nx, max(nc - 1, 1))),
+        dma((1,)),
+    ]
+    if with_ids:
+        scratch += [dma((nz,)), dma((max(nz - 1, 1),))]
+    out = pl.pallas_call(
+        functools.partial(gather_kernel, with_ids),
+        in_specs=[vmem, vmem] if with_ids else [vmem],
+        out_specs=[anywhere, vmem] if with_ids else anywhere,
+        out_shape=[shape, jax.ShapeDtypeStruct((nz,) + ids.shape, ids.dtype)] if with_ids else shape,
+        scratch_shapes=scratch,
+        compiler_params=pltpu.CompilerParams(collective_id=collective, has_side_effects=True),
+    )(*([own, ids] if with_ids else [own]))
+    depth = own.shape[1]
+    if with_ids:
+        return out[0].reshape(-1, depth), out[1].reshape(1, -1)
+    return out.reshape(-1, depth)
+
+
+def reduce_kernel(
+    part_ref, gain_ref, out_ref, mine, core_in, x_out, x_in, z_out, z_in,
+    local_sem, core_s, core_r, x_s, x_r, z_s, z_r,
+):
+    (z, x, c), (nz, nx, nc) = place()
+    f32 = jnp.float32
+    greet()
+    other = turn(c, 1, nc)
+    core, kept = [], []
+    for k in range(nz):
+        s = turn(z, k + 1, nz)
+        item = pltpu.make_async_remote_copy(
+            src_ref=part_ref.at[s, other],
+            dst_ref=core_in.at[k],
+            send_sem=core_s.at[k],
+            recv_sem=core_r.at[k],
+            device_id={"inner": other},
+            device_id_type=MESH,
+        )
+        item.start()
+        core.append(item)
+        stay = pltpu.make_async_copy(part_ref.at[s, c], mine.at[k], local_sem.at[k])
+        stay.start()
+        kept.append(stay)
+
+    def pair(k, xs):
+        return mine[k, xs].astype(f32) + core_in[k, xs].astype(f32)
+
+    across, along = [], []
+
+    def finish(k):
+        total = pair(k, x)
+        for step in range(1, nx):
+            across[k][step - 1].wait_recv()
+            total = total + x_in[k, step - 1].astype(f32)
+        if k == nz - 1:
+            return total
+        z_out[k] = total.astype(z_out.dtype)
+        item = pltpu.make_async_remote_copy(
+            src_ref=z_out.at[k],
+            dst_ref=z_in.at[k],
+            send_sem=z_s.at[k],
+            recv_sem=z_r.at[k],
+            device_id={"wide": turn(z, k + 1, nz)},
+            device_id_type=MESH,
+        )
+        item.start()
+        along.append(item)
+
+    for k in range(nz):
+        kept[k].wait()
+        core[k].wait_recv()
+        items = []
+        for step in range(1, nx):
+            xs = turn(x, step, nx)
+            x_out[k, step - 1] = pair(k, xs).astype(x_out.dtype)
+            item = pltpu.make_async_remote_copy(
+                src_ref=x_out.at[k, step - 1],
+                dst_ref=x_in.at[k, step - 1],
+                send_sem=x_s.at[k, step - 1],
+                recv_sem=x_r.at[k, step - 1],
+                device_id={"expert": xs},
+                device_id_type=MESH,
+            )
+            item.start()
+            items.append(item)
+        across.append(items)
+        if k > 0:
+            finish(k - 1)
+    total = finish(nz - 1)
+    for k in range(nz - 1):
+        along[k].wait_recv()
+        total = total + z_in[k].astype(f32)
+    center = jnp.mean(total, axis=1, keepdims=True)
+    spread = jnp.mean(jnp.square(total - center), axis=1, keepdims=True)
+    normed = (total - center) * lax.rsqrt(spread + 1e-05) * gain_ref[...].astype(f32)
+    out_ref[...] = normed.astype(out_ref.dtype)
+    for item in core + along + [i for items in across for i in items]:
+        item.wait_send()
+
+
+def run_reduce(part, gain, share, collective):
+    nz, nx, nc = (lax.axis_size(a) for a in ALL)
+    width = part.shape[1]
+    dma = pltpu.SemaphoreType.DMA
+    kind = part.dtype
+    part = part.reshape(nz, nc, nx, share, width)
+    few = max(nx - 1, 1)
+    vmem = pl.BlockSpec(memory_space=pltpu.VMEM)
+    return pl.pallas_call(
+        reduce_kernel,
+        in_specs=[pl.BlockSpec(memory_space=pl.ANY), vmem],
+        out_specs=vmem,
+        out_shape=jax.ShapeDtypeStruct((share, width), kind),
+        scratch_shapes=[
+            pltpu.VMEM((nz, nx, share, width), kind),
+            pltpu.VMEM((nz, nx, share, width), kind),
+            pltpu.VMEM((nz, few, share, width), kind),
+            pltpu.VMEM((nz, few, share, width), kind),
+            pltpu.VMEM((nz, share, width), kind),
+            pltpu.VMEM((nz, share, width), kind),
+            dma((nz,)),
+            dma((nz,)),
+            dma((nz,)),
+            dma((nz, few)),
+            dma((nz, few)),
+            dma((nz,)),
+            dma((nz,)),
+        ],
+        compiler_params=pltpu.CompilerParams(
+            collective_id=collective, has_side_effects=True, vmem_limit_bytes=VMEM_LIMIT
+        ),
+    )(part, gain)
 
 
 def expert_kernel(tasks, x_ref, gate_ref, win_ref, wout_ref, out_ref, acc_ref):
@@ -79,7 +339,7 @@
             pl.BlockSpec(expert_out.shape, lambda i: (0, 0, 0), pipeline_mode=pl.Buffered(1)),
         ],
         out_specs=pl.BlockSpec((block, tasks * width), lambda i: (i, 0)),
-        out_shape=jax.ShapeDtypeStruct((rows, tasks * width), jnp.float32),
+        out_shape=jax.ShapeDtypeStruct((rows, tasks * width), jnp.bfloat16),
         scratch_shapes=[pltpu.VMEM((block, tasks * width), jnp.float32)],
         compiler_params=pltpu.CompilerParams(vmem_limit_bytes=VMEM_LIMIT),
     )(x, gate_weight, expert_in, expert_out)
@@ -150,19 +410,15 @@
 ):
     rows = candidates.shape[0]
     tasks = task_weight.shape[1]
-    share = rows // (lax.axis_size("expert") * lax.axis_size("inner"))
-    spot = lax.axis_index("expert") * lax.axis_size("inner") + lax.axis_index("inner")
+    nx, nc = lax.axis_size("expert"), lax.axis_size("inner")
+    share = rows // (nx * nc)
+    spot = lax.axis_index("inner") * nx + lax.axis_index("expert")
     wide = lax.axis_index("wide")
-    requests = lax.all_gather(request_of, "wide", axis=0, tiled=True)
     quarter = lax.dynamic_slice_in_dim(candidates, spot * share, share, 0)
-    everyone = lax.all_gather(quarter, ALL, axis=0, tiled=True)
+    everyone, requests = run_gather(quarter, request_of[None, :], 0)
     partial_mix = run_experts(everyone, gate_weight, expert_in, expert_out, tasks)
-    mixed = lax.psum_scatter(partial_mix, ALL, scatter_dimension=0, tiled=True)
-    center = jnp.mean(mixed, axis=1, keepdims=True)
-    spread = jnp.mean(jnp.square(mixed - center), axis=1, keepdims=True)
-    gain = norm_gain.astype(jnp.float32)
-    normed = ((mixed - center) * lax.rsqrt(spread + 1e-05) * gain).astype(jnp.bfloat16)
-    normed_all = lax.all_gather(normed, ALL, axis=0, tiled=True)
+    normed = run_reduce(partial_mix, norm_gain[None, :], share, 1)
+    normed_all = run_gather(normed, None, 2)
     own = lax.dynamic_slice_in_dim(normed_all, wide * rows, rows, 0)
     queries = jnp.dot(own, query_weight, preferred_element_type=jnp.float32).astype(jnp.bfloat16)
     keys = jnp.dot(normed_all, key_weight, preferred_element_type=jnp.float32).astype(jnp.bfloat16)
@@ -170,7 +426,7 @@
         jnp.bfloat16
     )
     term = run_attention(
-        queries, keys, values, request_of[:, None], requests[None, :], attn_weight
+        queries, keys, values, request_of[:, None], requests, attn_weight
     )
     attention = lax.psum(term, ("expert", "inner"))
     return jnp.dot(own, task_weight, preferred_element_type=jnp.float32) + attention

time: 328 us -> 240 us (0.73)
  waiting for transfers between devices: 194 us -> 0 us
  Pallas kernels: 76.4 us -> 210 us
  between operations: 13.2 us -> 0.1 us
  blocking collectives: 23.5 us -> 13.8 us
  other arithmetic: 4.32 us -> 0 us
    pallas_call x0 -> x3, Pallas kernels: none -> 133 us  [the longest x2 97 us: run_gather(): pl.pallas_call(functools.partial(gather_kernel, with_ids), in_specs=[vmem...]
    reduce_scatter x1 -> x0, waiting for transfers between devices: 101 us -> none  [local(): mixed = lax.psum_scatter(partial_mix, ALL, scatter_dimension=0, tiled=True)]
    all_gather x2 -> x0, waiting for transfers between devices: 92.9 us -> none  [the longest x1 53 us: local(): everyone = lax.all_gather(quarter, ALL, axis=0, tiled=True)]
    all_gather x1 -> x0, blocking collectives: 9.32 us -> none  [local(): requests = lax.all_gather(request_of, 'wide', axis=0, tiled=True)]
  transfers between devices with their start and end apart: 3 -> 0, of which waited for: 3 -> 0; matrix products, arithmetic and copies ran while one was open for 0% -> 0% of each run, Pallas kernels for 0% -> 0%
where the time goes in v2:
time: 240 us; the launch traced here: 239 us
  Pallas kernels  210 us (88%)
  blocking collectives  13.8 us (6%)
  matrix products  10.9 us (5%)
  local copies, waits for them, and re-layouts  4.9 us (2%)
    pallas_call x2, Pallas kernels, run_gather(): pl.pallas_call(functools.partial(gather_kernel, with_ids), in_specs=[vmem...  97 us
    pallas_call x1, Pallas kernels, run_experts(): pl.pallas_call(functools.partial(expert_kernel, tasks), grid=(rows // blo...  62.7 us
    pallas_call x1, Pallas kernels, run_reduce(): pl.pallas_call(reduce_kernel, in_specs=[pl.BlockSpec(memory_space=pl.ANY)...  36.4 us
    psum x1, blocking collectives, local(): attention = lax.psum(term, ('expert', 'inner'))  13.8 us
    pallas_call x1, Pallas kernels, run_attention(): pl.pallas_call(attention_kernel, grid=(rows // block,), in_specs=[pl.Bloc...  13.6 us

profile of v2, /device:TPU:9, one launch (start us, length us, event | category | flops | bytes accessed | tf_op | source)
XLA Modules:
  0.0 239.3 jit_solution(14760114907982479674)
XLA Ops:
  0.0 0.0 copy-start
  0.0 1.2 copy-done
  1.2 0.7 constant_dynamic-slice_fusion.refs_0_
  1.9 49.4 %shard_map.109 = (bf16[4,2,2,128,1024]{4,3,2,1,0:T(8,128)(2,1)}, s32[4,1,512]{2,1,0:T(1,128)}) custom-call(bf16[128,1024]{1,0:T(8,128)(2,1)} %constant_dynamic-slice_fusion.refs_0_, s32[1,512]{1,0:T(1,128)} %bitcast.19), custom_call_target="tpu_custom_call" | custom-call | tf_op jit(solution)/shard_map/pallas_call | solution.py:147
  51.3 0.0 copy-start.4
  51.3 62.7 %shard_map.110 = bf16[2048,1024]{1,0:T(8,128)(2,1)} custom-call(bf16[2048,1024]{1,0:T(8,128)(2,1)} %bitcast.17, bf16[1024,128]{1,0:T(8,128)(2,1)} %gate_ref.1, bf16[16,1024,256]{2,1,0:T(8,128)(2,1)} %win_ref.1, bf16[16,256,256]{2,1,0:T(8,128)(2,1)} %wout_ref.1), custom_call_target="tpu_custom_call" | custom-call | tf_op jit(solution)/shard_map/pallas_call | solution.py:332
  114.0 0.0 copy-done.4
  114.0 0.6 broadcast_in_dim.10.gain_ref
  114.6 0.0 copy-start.6
  114.6 36.4 %shard_map.111.refs_0_ = bf16[128,1024]{1,0:T(8,128)(2,1)} custom-call(bf16[4,2,2,128,1024]{4,3,2,1,0:T(8,128)(2,1)} %bitcast.12, bf16[1,1024]{1,0:T(2,128)(2,1)} %broadcast_in_dim.10.gain_ref), custom_call_target="tpu_custom_call" | custom-call | tf_op jit(solution)/shard_map/pallas_call | solution.py:250
  151.0 0.0 copy-start.7
  151.0 47.6 %shard_map.112 = bf16[4,2,2,128,1024]{4,3,2,1,0:T(8,128)(2,1)} custom-call(bf16[128,1024]{1,0:T(8,128)(2,1)} %shard_map.111.refs_0_), custom_call_target="tpu_custom_call" | custom-call | tf_op jit(solution)/shard_map/pallas_call | solution.py:147
  198.7 0.0 copy-done.6
  198.7 2.4 convolution_convert_fusion.2.q_ref
  201.1 0.0 copy-done.7
  201.1 0.0 copy-start.1
  201.1 0.0 copy-start.8
  201.1 4.6 %convolution_convert_fusion.v_ref = bf16[2048,256]{1,0:T(8,128)(2,1)} fusion(bf16[2048,1024]{1,0:T(8,128)(2,1)} %bitcast.14, bf16[1024,256]{1,0:T(8,128)(2,1)S(1)} %copy-done.7), kind=kOutput, calls=%fused_computation | convolution fusion | flops 1074266112 | bytes 5767168 | tf_op jit(solution)/shard_map/dot_general | solution.py:425
  205.7 0.0 copy-done.1
  205.7 0.0 copy-done.8
  205.7 0.0 copy-start.3
  205.7 0.0 copy-start.2
  205.7 2.2 convolution_convert_fusion.1.k_ref
  207.9 0.0 copy-done.3
  207.9 0.9 copy.19.own_ref
  208.8 0.0 copy-done.5
  208.8 0.7 copy.20.weight_ref
  209.6 13.6 %shard_map.113 = f32[512,4]{1,0:T(8,128)} custom-call(bf16[512,256]{1,0:T(8,128)(2,1)} %convolution_convert_fusion.2.q_ref, bf16[2048,256]{1,0:T(8,128)(2,1)} %convolution_convert_fusion.1.k_ref, bf16[2048,256]{1,0:T(8,128)(2,1)} %convolution_convert_fusion.v_ref, s32[512,1]{1,0:T(8,128)} %copy.19.own_ref, s32[1,2048]{1,0:T(1,128)} %bitcast.18, ...), custom_call_target="tpu_custom_call" | custom-call | tf_op jit(solution)/shard_map/pallas_call | solution.py:381
  223.1 13.8 %psum.7 = f32[512,4]{1,0:T(8,128)S(1)} all-reduce(f32[512,4]{1,0:T(8,128)} %shard_map.113), channel_id=1, replica_groups=mesh['groups'=2,'wide'=4,'expert'=2,'inner'=2] {'expert','inner'}, use_global_device_ids=true, to_apply=%region_0.0 | all-reduce | flops 2048 | bytes 16384 | tf_op jit(solution)/shard_map/psum | solution.py:431
  236.9 0.0 copy-done.2
  236.9 1.6 convolution_add_fusion
  238.6 0.7 copy.22
  (1 shorter events, 0.0 us)
Async XLA Ops:
  0.0 1.2 copy-start
  51.3 62.7 %copy-start.4 = (bf16[1024]{0:T(1024)(128)(2,1)S(1)}, bf16[1024]{0:T(1024)(128)(2,1)}, u32[]{:S(2)}) copy-start(bf16[1024]{0:T(1024)(128)(2,1)} %param.15) | copy-start | bytes 6148
  114.6 84.1 %copy-start.6 = (bf16[1024,256]{1,0:T(8,128)(2,1)S(1)}, bf16[1024,256]{1,0:T(8,128)(2,1)}, u32[]{:S(2)}) copy-start(bf16[1024,256]{1,0:T(8,128)(2,1)} %param.16) | copy-start | bytes 1572868
  151.0 50.0 %copy-start.7 = (bf16[1024,256]{1,0:T(8,128)(2,1)S(1)}, bf16[1024,256]{1,0:T(8,128)(2,1)}, u32[]{:S(2)}) copy-start(bf16[1024,256]{1,0:T(8,128)(2,1)} %param.18) | copy-start | bytes 1572868
  201.1 4.6 %copy-start.1 = (bf16[4,2,2,128,1024]{4,3,2,1,0:T(8,128)(2,1)S(1)}, bf16[4,2,2,128,1024]{4,3,2,1,0:T(8,128)(2,1)}, u32[]{:S(2)}) copy-start(bf16[4,2,2,128,1024]{4,3,2,1,0:T(8,128)(2,1)} %shard_map.112) | copy-start | bytes 12582916
  201.1 4.6 %copy-start.8 = (bf16[1024,256]{1,0:T(8,128)(2,1)S(1)}, bf16[1024,256]{1,0:T(8,128)(2,1)}, u32[]{:S(2)}) copy-start(bf16[1024,256]{1,0:T(8,128)(2,1)} %param.17) | copy-start | bytes 1572868
  205.7 2.3 copy-start.3
  205.7 3.1 %copy-start.5 = (bf16[256,4]{0,1:T(4,128)(2,1)S(1)}, bf16[256,4]{0,1:T(4,128)(2,1)}, u32[]{:S(2)}) copy-start(bf16[256,4]{0,1:T(4,128)(2,1)} %param.20) | copy-start | bytes 6148
  205.7 31.2 %copy-start.2 = (bf16[1024,4]{0,1:T(4,128)(2,1)S(1)}, bf16[1024,4]{0,1:T(4,128)(2,1)}, u32[]{:S(2)}) copy-start(bf16[1024,4]{0,1:T(4,128)(2,1)} %param.19) | copy-start | bytes 24580

commit v3 on v2

--- a/solution.py
+++ b/solution.py
@@ -328,7 +328,7 @@
     rows, depth = x.shape
     held, _, units = expert_in.shape
     width = expert_out.shape[1]
-    block = min(256, rows)
+    block = min(512, rows)
     return pl.pallas_call(
         functools.partial(expert_kernel, tasks),
         grid=(rows // block,),
@@ -428,7 +428,7 @@
     term = run_attention(
         queries, keys, values, request_of[:, None], requests, attn_weight
     )
-    attention = lax.psum(term, ("expert", "inner"))
+    attention = lax.psum(term.T, ("expert", "inner")).T
     return jnp.dot(own, task_weight, preferred_element_type=jnp.float32) + attention
 
 

time: 240 us -> 230 us (0.958)
  Pallas kernels: 210 us -> 200 us
    pallas_call x1, Pallas kernels: 62.7 us -> 52.6 us  [run_experts(): pl.pallas_call(functools.partial(expert_kernel, tasks), grid=(rows // blo...]
where the time goes in v3:
time: 230 us; the launch traced here: 229 us
  Pallas kernels  200 us (87%)
  blocking collectives  13.8 us (6%)
  matrix products  10.8 us (5%)
  local copies, waits for them, and re-layouts  4.9 us (2%)
    pallas_call x2, Pallas kernels, run_gather(): pl.pallas_call(functools.partial(gather_kernel, with_ids), in_specs=[vmem...  97 us
    pallas_call x1, Pallas kernels, run_experts(): pl.pallas_call(functools.partial(expert_kernel, tasks), grid=(rows // blo...  52.6 us
    pallas_call x1, Pallas kernels, run_reduce(): pl.pallas_call(reduce_kernel, in_specs=[pl.BlockSpec(memory_space=pl.ANY)...  36.4 us
    psum x1, blocking collectives, local(): attention = lax.psum(term.T, ('expert', 'inner')).T  13.8 us
    pallas_call x1, Pallas kernels, run_attention(): pl.pallas_call(attention_kernel, grid=(rows // block,), in_specs=[pl.Bloc...  13.6 us
    dot_general x1, matrix products, local(): jnp.dot(normed_all, value_weight, preferred_element_type=jnp.float32)  4.6 us

profile of v3, /device:TPU:9, one launch (start us, length us, event | category | flops | bytes accessed | tf_op | source)
XLA Modules:
  0.0 229.2 jit_solution(15663877670151047881)
XLA Ops:
  0.0 0.0 copy-start
  0.0 1.2 copy-done
  1.2 0.7 constant_dynamic-slice_fusion.refs_0_
  1.9 49.4 %shard_map.109 = (bf16[4,2,2,128,1024]{4,3,2,1,0:T(8,128)(2,1)}, s32[4,1,512]{2,1,0:T(1,128)}) custom-call(bf16[128,1024]{1,0:T(8,128)(2,1)} %constant_dynamic-slice_fusion.refs_0_, s32[1,512]{1,0:T(1,128)} %bitcast.19), custom_call_target="tpu_custom_call" | custom-call | tf_op jit(solution)/shard_map/pallas_call | solution.py:147
  51.3 0.0 copy-start.4
  51.3 52.6 %shard_map.110 = bf16[2048,1024]{1,0:T(8,128)(2,1)} custom-call(bf16[2048,1024]{1,0:T(8,128)(2,1)} %bitcast.17, bf16[1024,128]{1,0:T(8,128)(2,1)} %gate_ref.1, bf16[16,1024,256]{2,1,0:T(8,128)(2,1)} %win_ref.1, bf16[16,256,256]{2,1,0:T(8,128)(2,1)} %wout_ref.1), custom_call_target="tpu_custom_call" | custom-call | tf_op jit(solution)/shard_map/pallas_call | solution.py:332
  104.0 0.0 copy-done.4
  104.0 0.6 broadcast_in_dim.10.gain_ref
  104.6 0.0 copy-start.6
  104.6 36.4 %shard_map.111.refs_0_ = bf16[128,1024]{1,0:T(8,128)(2,1)} custom-call(bf16[4,2,2,128,1024]{4,3,2,1,0:T(8,128)(2,1)} %bitcast.12, bf16[1,1024]{1,0:T(2,128)(2,1)} %broadcast_in_dim.10.gain_ref), custom_call_target="tpu_custom_call" | custom-call | tf_op jit(solution)/shard_map/pallas_call | solution.py:250
  141.0 0.0 copy-start.7
  141.0 47.7 %shard_map.112 = bf16[4,2,2,128,1024]{4,3,2,1,0:T(8,128)(2,1)} custom-call(bf16[128,1024]{1,0:T(8,128)(2,1)} %shard_map.111.refs_0_), custom_call_target="tpu_custom_call" | custom-call | tf_op jit(solution)/shard_map/pallas_call | solution.py:147
  188.7 0.0 copy-done.6
  188.7 2.4 %convolution_convert_fusion.2.q_ref = bf16[512,256]{1,0:T(8,128)(2,1)} fusion(bf16[1024,256]{1,0:T(8,128)(2,1)S(1)} %copy-done.6, bf16[2048,1024]{1,0:T(8,128)(2,1)} %bitcast.13, s32[]{:T(128)S(6)} %select_n.7), kind=kOutput, calls=%fused_computation.2 | convolution fusion | flops 268566528 | bytes 1835012 | tf_op jit(solution)/shard_map/dot_general | solution.py:423
  191.0 0.0 copy-done.7
  191.0 0.0 copy-start.1
  191.0 0.0 copy-start.8
  191.0 4.6 %convolution_convert_fusion.v_ref = bf16[2048,256]{1,0:T(8,128)(2,1)} fusion(bf16[2048,1024]{1,0:T(8,128)(2,1)} %bitcast.14, bf16[1024,256]{1,0:T(8,128)(2,1)S(1)} %copy-done.7), kind=kOutput, calls=%fused_computation | convolution fusion | flops 1074266112 | bytes 5767168 | tf_op jit(solution)/shard_map/dot_general | solution.py:425
  195.6 0.0 copy-done.1
  195.6 0.0 copy-done.8
  195.6 0.0 copy-start.3
  195.6 0.0 copy-start.2
  195.7 2.2 convolution_convert_fusion.1.k_ref
  197.9 0.0 copy-done.3
  197.9 0.9 copy.19.own_ref
  198.8 0.0 copy-done.5
  198.8 0.7 copy.20.weight_ref
  199.5 13.6 %shard_map.113 = f32[512,4]{1,0:T(8,128)} custom-call(bf16[512,256]{1,0:T(8,128)(2,1)} %convolution_convert_fusion.2.q_ref, bf16[2048,256]{1,0:T(8,128)(2,1)} %convolution_convert_fusion.1.k_ref, bf16[2048,256]{1,0:T(8,128)(2,1)} %convolution_convert_fusion.v_ref, s32[512,1]{1,0:T(8,128)} %copy.19.own_ref, s32[1,2048]{1,0:T(1,128)} %bitcast.18, ...), custom_call_target="tpu_custom_call" | custom-call | tf_op jit(solution)/shard_map/pallas_call | solution.py:381
  213.1 13.8 %psum.7 = f32[512,4]{1,0:T(8,128)S(1)} all-reduce(f32[512,4]{1,0:T(8,128)} %shard_map.113), channel_id=1, replica_groups=mesh['groups'=2,'wide'=4,'expert'=2,'inner'=2] {'expert','inner'}, use_global_device_ids=true, to_apply=%region_0.0 | all-reduce | flops 2048 | bytes 16384 | tf_op jit(solution)/shard_map/psum | solution.py:431
  226.9 0.0 copy-done.2
  226.9 1.6 convolution_add_fusion
  228.5 0.7 copy.22
  (1 shorter events, 0.0 us)
Async XLA Ops:
  0.0 1.2 copy-start
  51.3 52.7 %copy-start.4 = (bf16[1024]{0:T(1024)(128)(2,1)S(1)}, bf16[1024]{0:T(1024)(128)(2,1)}, u32[]{:S(2)}) copy-start(bf16[1024]{0:T(1024)(128)(2,1)} %param.15) | copy-start | bytes 6148
  104.6 84.1 %copy-start.6 = (bf16[1024,256]{1,0:T(8,128)(2,1)S(1)}, bf16[1024,256]{1,0:T(8,128)(2,1)}, u32[]{:S(2)}) copy-start(bf16[1024,256]{1,0:T(8,128)(2,1)} %param.16) | copy-start | bytes 1572868
  141.0 50.0 %copy-start.7 = (bf16[1024,256]{1,0:T(8,128)(2,1)S(1)}, bf16[1024,256]{1,0:T(8,128)(2,1)}, u32[]{:S(2)}) copy-start(bf16[1024,256]{1,0:T(8,128)(2,1)} %param.18) | copy-start | bytes 1572868
  191.0 4.6 %copy-start.1 = (bf16[4,2,2,128,1024]{4,3,2,1,0:T(8,128)(2,1)S(1)}, bf16[4,2,2,128,1024]{4,3,2,1,0:T(8,128)(2,1)}, u32[]{:S(2)}) copy-start(bf16[4,2,2,128,1024]{4,3,2,1,0:T(8,128)(2,1)} %shard_map.112) | copy-start | bytes 12582916
  191.0 4.6 %copy-start.8 = (bf16[1024,256]{1,0:T(8,128)(2,1)S(1)}, bf16[1024,256]{1,0:T(8,128)(2,1)}, u32[]{:S(2)}) copy-start(bf16[1024,256]{1,0:T(8,128)(2,1)} %param.17) | copy-start | bytes 1572868
  195.6 2.3 copy-start.3
  195.6 3.1 %copy-start.5 = (bf16[256,4]{0,1:T(4,128)(2,1)S(1)}, bf16[256,4]{0,1:T(4,128)(2,1)}, u32[]{:S(2)}) copy-start(bf16[256,4]{0,1:T(4,128)(2,1)} %param.20) | copy-start | bytes 6148
  195.6 31.2 %copy-start.2 = (bf16[1024,4]{0,1:T(4,128)(2,1)S(1)}, bf16[1024,4]{0,1:T(4,128)(2,1)}, u32[]{:S(2)}) copy-start(bf16[1024,4]{0,1:T(4,128)(2,1)} %param.19) | copy-start | bytes 24580
